TPU v7x, 32 devices: a whole 2x2x4 slice. The times are simulated.
32 devices in a mesh: depth: 4 (over z), row: 4 (over x, core), col: 2 (over y).
Axes of the slice: x: 2, y: 2, z: 4, core: 2. Of those that a mesh axis runs over, the one named last changes fastest.
Arguments:
- acts: bfloat16 [2048, 4096], P(('depth', 'col'), 'row'), may hold values from -0.3125 to 0.3125
- grad_out: bfloat16 [2048, 14336], P(('depth', 'row'), 'col'), may hold values from -6 to 6
- weight: bfloat16 [4096, 14336], P('row', 'col'), may hold values from -0.046875 to 0.046875
Outputs:
- grad_acts: bfloat16 [2048, 4096], P(('depth', 'col'), 'row')
- grad_weight: bfloat16 [4096, 14336], P('row', 'col')
All inputs are finite; a program needn't handle non-finite values.
Results may differ from a plain program's by a relative error of at most 0.013.
Values may be sent and summed in bfloat16 or wider, within the bound.
A program may use at most 128 MiB of HBM per device.

v0:
```python
import jax
import jax.numpy as jnp
from jax import lax
from jax.sharding import PartitionSpec as P


def shards(acts, grad_out, weight):
    grad_rows = lax.all_gather(grad_out, "row", axis=0, tiled=True)
    grad_acts = lax.psum_scatter(
        lax.dot_general(
            grad_rows, weight, (((1,), (1,)), ((), ())), preferred_element_type=jnp.float32
        ).astype(jnp.bfloat16),
        "col",
        scatter_dimension=0,
        tiled=True,
    )
    partial_sum = lax.dot_general(
        lax.all_gather(acts, "col", axis=0, tiled=True),
        grad_rows,
        (((0,), (0,)), ((), ())),
        preferred_element_type=jnp.float32,
    )
    grad_weight = lax.psum(partial_sum.astype(jnp.bfloat16), "depth")
    return (grad_acts, grad_weight)


def solution(mesh):
    in_specs = (P(("depth", "col"), "row"), P(("depth", "row"), "col"), P("row", "col"))
    out_specs = (P(("depth", "col"), "row"), P("row", "col"))
    return jax.shard_map(shards, mesh=mesh, in_specs=in_specs, out_specs=out_specs, check_vma=False)
```

profile of v0, /device:TPU:0, one launch (start us, length us, event | category | flops | bytes accessed | tf_op | source)
XLA Modules:
  0.0 627.1 jit_solution(1887198143985389784)
XLA Ops:
  7.2 0.0 all-gather.3.cloned.1.call-start
  7.2 0.7 all-gather.3.cloned.1.call-update
  7.9 0.0 all-gather.5.cloned.1.call-start
  7.9 0.7 all-gather.5.cloned.1.call-update
  8.6 0.0 reduce-scatter.2.cloned.1.call-start
  8.7 55.9 %all-gather.3.cloned.1.call-done = bf16[512,7168]{1,0:T(8,128)(2,1)} async-done(((bf16[128,7168]{1,0:T(8,128)(2,1)}), bf16[512,7168]{1,0:T(8,128)(2,1)}) %all-gather.3.cloned.1.call-update) | async-done | bytes 7340048 | tf_op jit(solution)/shard_map/all_gather | solution.py:8
  64.6 14.0 %convolution_convert_fusion.1 = bf16[512,1024]{1,0:T(8,128)(2,1)} fusion(bf16[512,7168]{1,0:T(8,128)(2,1)} %all-gather.3.cloned.1.call-done, bf16[1024,7168]{1,0:T(8,128)(2,1)} %param.5), kind=kOutput, calls=%fused_computation.1 | convolution fusion | flops 7516717056 | bytes 23068672 | tf_op jit(solution)/shard_map/dot_general | solution.py:10
  78.6 0.0 reduce-scatter.2.cloned.1.call-update
  78.6 0.0 all-reduce.2.cloned.1.call-start
  78.7 8.8 %all-gather.5.cloned.1.call-done = bf16[512,1024]{1,0:T(8,128)(2,1)} async-done(((bf16[256,1024]{1,0:T(8,128)(2,1)}), bf16[512,1024]{1,0:T(8,128)(2,1)}) %all-gather.5.cloned.1.call-update) | async-done | bytes 1048592 | tf_op jit(solution)/shard_map/all_gather | solution.py:18
  87.5 13.4 %convolution_convert_fusion = bf16[1024,7168]{1,0:T(8,128)(2,1)} fusion(bf16[512,1024]{1,0:T(8,128)(2,1)} %all-gather.5.cloned.1.call-done, bf16[512,7168]{1,0:T(8,128)(2,1)} %all-gather.3.cloned.1.call-done), kind=kOutput, calls=%fused_computation | convolution fusion | flops 7523532800 | bytes 23068672 | tf_op jit(solution)/shard_map/dot_general | solution.py:17
  100.9 0.0 all-reduce.2.cloned.1.call-update
  100.9 9.8 %reduce-scatter.2.cloned.1.call-done = bf16[256,1024]{1,0:T(8,128)(2,1)} async-done(((bf16[512,1024]{1,0:T(8,128)(2,1)}), bf16[256,1024]{1,0:T(8,128)(2,1)}) %reduce-scatter.2.cloned.1.call-update) | async-done | bytes 524304 | tf_op jit(solution)/shard_map/reduce_scatter | solution.py:9
  110.7 496.7 %all-reduce.2.cloned.1.call-done = bf16[1024,7168]{1,0:T(8,128)(2,1)} async-done(((bf16[1024,7168]{1,0:T(8,128)(2,1)}), bf16[1024,7168]{1,0:T(8,128)(2,1)}) %all-reduce.2.cloned.1.call-update) | async-done | bytes 14680080 | tf_op jit(solution)/shard_map/psum | solution.py:23
  607.4 13.2 %copy.6 = bf16[1024,7168]{1,0:T(8,128)(2,1)} copy(bf16[1024,7168]{1,0:T(8,128)(2,1)} %all-reduce.2.cloned.1.call-done) | data formatting | bytes 29360128
Async XLA Ops:
  7.2 57.4 %all-gather.3.cloned.1.call-start = ((), (), s32[]{:S(2)}) async-start(), calls=%async_computation.1 | async-start | bytes 9175040 | tf_op jit(solution)/shard_map/all_gather | solution.py:8
  7.9 79.6 %all-gather.5.cloned.1.call-start = ((), (), s32[]{:S(2)}) async-start(), calls=%async_computation.3 | async-start | bytes 1572864 | tf_op jit(solution)/shard_map/all_gather | solution.py:18
  8.6 102.0 %reduce-scatter.2.cloned.1.call-start = ((), (), s32[]{:S(2)}) async-start(), calls=%async_computation.2 | async-start | bytes 1572864 | tf_op jit(solution)/shard_map/reduce_scatter | solution.py:9
  78.6 528.8 %all-reduce.2.cloned.1.call-start = ((), (), s32[]{:S(2)}) async-start(), calls=%async_computation.4 | async-start | bytes 29360128 | tf_op jit(solution)/shard_map/psum | solution.py:23
Sparse Core Ops, SparseCore 0:
  9.5 55.0 all-gather.2
  66.1 21.2 all-gather.4
  90.3 20.3 reduce-scatter.1
  113.6 493.7 all-reduce.1
where the time goes:
time: 627 us
  waiting for transfers between devices  573 us (91%)
  matrix products  27.4 us (4%)
  between operations  13.8 us (2%)
  local copies, waits for them, and re-layouts  13.2 us (2%)
    psum x1, waiting for transfers between devices, shards(): grad_weight = lax.psum(partial_sum.astype(jnp.bfloat16), 'depth')  497 us
    all_gather x1, waiting for transfers between devices, shards(): grad_rows = lax.all_gather(grad_out, 'row', axis=0, tiled=True)  55.9 us
    dot_general x1, matrix products, shards(): lax.dot_general(grad_rows, weight, (((1,), (1,)), ((), ())), preferred_el...  14 us
    dot_general x1, matrix products, shards(): lax.dot_general(lax.all_gather(acts, 'col', axis=0, tiled=True), grad_row...  13.4 us
    unnamed x1, local copies, waits for them, and re-layouts  13.2 us
  transfers between devices with their start and end apart: 4, of which 4 were waited for; matrix products, arithmetic and copies ran while one was open for 4% of the time, Pallas kernels for 0%

commit v1 on v0

--- a/solution.py
+++ b/solution.py
@@ -20,7 +20,7 @@
         (((0,), (0,)), ((), ())),
         preferred_element_type=jnp.float32,
     )
-    grad_weight = lax.psum(partial_sum.astype(jnp.bfloat16), "depth")
+    grad_weight = jnp.sum(lax.all_gather(partial_sum.astype(jnp.bfloat16), "depth"), axis=0)
     return (grad_acts, grad_weight)
 
 

time: 627 us -> 1110 us (1.77)
  waiting for transfers between devices: 573 us -> 1040 us
  other arithmetic: 0 us -> 28 us
  local copies, waits for them, and re-layouts: 13.2 us -> 0 us
    all_gather x0 -> x1, waiting for transfers between devices: none -> 960 us  [shards(): lax.all_gather(partial_sum.astype(jnp.bfloat16), 'depth')]
    psum x1 -> x0, waiting for transfers between devices: 497 us -> none  [shards(): grad_weight = lax.psum(partial_sum.astype(jnp.bfloat16), 'depth')]
    reduce_sum x0 -> x1, other arithmetic: none -> 28 us  [shards(): jnp.sum(lax.all_gather(partial_sum.astype(jnp.bfloat16), 'depth'), axis=0)]
    all_gather x1, waiting for transfers between devices: 8.8 us -> 24.9 us  [shards(): lax.all_gather(acts, 'col', axis=0, tiled=True)]
    unnamed x1 -> x0, local copies, waits for them, and re-layouts: 13.2 us -> none
  transfers between devices with their start and end apart: 4 -> 4, of which waited for: 4 -> 3; matrix products, arithmetic and copies ran while one was open for 4% -> 4% of each run, Pallas kernels for 0% -> 0%
where the time goes in v1:
time: 1110 us
  waiting for transfers between devices  1040 us (94%)
  other arithmetic  28 us (3%)
  matrix products  27.4 us (2%)
  between operations  13.8 us (1%)
    all_gather x1, waiting for transfers between devices, shards(): lax.all_gather(partial_sum.astype(jnp.bfloat16), 'depth')  960 us
    all_gather x1, waiting for transfers between devices, shards(): grad_rows = lax.all_gather(grad_out, 'row', axis=0, tiled=True)  53.9 us
    reduce_sum x1, other arithmetic, shards(): jnp.sum(lax.all_gather(partial_sum.astype(jnp.bfloat16), 'depth'), axis=0)  28 us
    all_gather x1, waiting for transfers between devices, shards(): lax.all_gather(acts, 'col', axis=0, tiled=True)  24.9 us
  transfers between devices with their start and end apart: 4, of which 3 were waited for; matrix products, arithmetic and copies ran while one was open for 4% of the time, Pallas kernels for 0%

profile of v1, /device:TPU:0, one launch (start us, length us, event | category | flops | bytes accessed | tf_op | source)
XLA Modules:
  0.0 1110.0 jit_solution(5795844557770253751)
XLA Ops:
  7.2 0.0 all-gather.7.cloned.1.call-start
  7.2 0.7 all-gather.7.cloned.1.call-update
  7.9 0.0 all-gather.5.cloned.1.call-start
  7.9 0.7 all-gather.5.cloned.1.call-update
  8.6 0.0 all-gather.9.cloned.1.call-start
  8.7 24.9 %all-gather.7.cloned.1.call-done = bf16[512,1024]{1,0:T(8,128)(2,1)} async-done(((bf16[256,1024]{1,0:T(8,128)(2,1)}), bf16[512,1024]{1,0:T(8,128)(2,1)}) %all-gather.7.cloned.1.call-update) | async-done | bytes 1048592 | tf_op jit(solution)/shard_map/all_gather | solution.py:18
  33.6 53.9 %all-gather.5.cloned.1.call-done = bf16[512,7168]{1,0:T(8,128)(2,1)} async-done(((bf16[128,7168]{1,0:T(8,128)(2,1)}), bf16[512,7168]{1,0:T(8,128)(2,1)}) %all-gather.5.cloned.1.call-update) | async-done | bytes 7340048 | tf_op jit(solution)/shard_map/all_gather | solution.py:8
  87.5 13.4 %convolution_convert_fusion = bf16[1024,7168]{1,0:T(8,128)(2,1)} fusion(bf16[512,1024]{1,0:T(8,128)(2,1)} %all-gather.7.cloned.1.call-done, bf16[512,7168]{1,0:T(8,128)(2,1)} %all-gather.5.cloned.1.call-done), kind=kOutput, calls=%fused_computation | convolution fusion | flops 7523532800 | bytes 23068672 | tf_op jit(solution)/shard_map/dot_general | solution.py:17
  100.9 0.0 all-gather.9.cloned.1.call-update
  100.9 0.0 reduce-scatter.2.cloned.1.call-start
  101.0 14.0 %convolution_convert_fusion.1 = bf16[512,1024]{1,0:T(8,128)(2,1)} fusion(bf16[512,7168]{1,0:T(8,128)(2,1)} %all-gather.5.cloned.1.call-done, bf16[1024,7168]{1,0:T(8,128)(2,1)} %param.5), kind=kOutput, calls=%fused_computation.1 | convolution fusion | flops 7516717056 | bytes 23068672 | tf_op jit(solution)/shard_map/dot_general | solution.py:10
  115.0 0.0 reduce-scatter.2.cloned.1.call-update
  115.0 960.5 %all-gather.9.cloned.1.call-done = bf16[4096,7168]{1,0:T(8,128)(2,1)} async-done(((bf16[1024,7168]{1,0:T(8,128)(2,1)}), bf16[4096,7168]{1,0:T(8,128)(2,1)}) %all-gather.9.cloned.1.call-update) | async-done | bytes 58720272 | tf_op jit(solution)/shard_map/all_gather | solution.py:23
  1075.5 28.0 %reduce_sum.12 = bf16[1024,7168]{1,0:T(8,128)(2,1)} reduce(bf16[4,1024,7168]{2,1,0:T(8,128)(2,1)} %bitcast.5, bf16[]{:T(256)} %constant.2.clone.1), dimensions={0}, to_apply=%region_1.0 | reduce | flops 22020096 | bytes 73400320 | tf_op jit(solution)/shard_map/reduce_sum | solution.py:23
  1103.4 0.0 reduce-scatter.2.cloned.1.call-done
Async XLA Ops:
  7.2 26.4 %all-gather.7.cloned.1.call-start = ((), (), s32[]{:S(2)}) async-start(), calls=%async_computation.3 | async-start | bytes 1572864 | tf_op jit(solution)/shard_map/all_gather | solution.py:18
  7.9 79.6 %all-gather.5.cloned.1.call-start = ((), (), s32[]{:S(2)}) async-start(), calls=%async_computation.1 | async-start | bytes 9175040 | tf_op jit(solution)/shard_map/all_gather | solution.py:8
  8.6 1066.8 %all-gather.9.cloned.1.call-start = ((), (), s32[]{:S(2)}) async-start(), calls=%async_computation.4 | async-start | bytes 73400320 | tf_op jit(solution)/shard_map/all_gather | solution.py:23
  100.9 1002.5 %reduce-scatter.2.cloned.1.call-start = ((), (), s32[]{:S(2)}) async-start(), calls=%async_computation.2 | async-start | bytes 1572864 | tf_op jit(solution)/shard_map/reduce_scatter | solution.py:9
Sparse Core Ops, SparseCore 0:
  9.5 23.9 all-gather.6
  35.1 52.2 all-gather.4
  101.0 974.3 all-gather.8
  1078.1 18.5 reduce-scatter.1
